TPU v7x, 128 devices: a whole 4x4x4 slice. The times are simulated.
128 devices in a mesh: group: 2 (over x_hi), dev: 64 (over z, x_lo, y, core).
Axes of the slice: x: 4 (x_hi: 2, x_lo: 2; x = x_hi * 2 + x_lo), y: 4, z: 4, core: 2. Of those that a mesh axis runs over, the one named last changes fastest.
Arguments:
- query_latent: bfloat16 [512, 128, 512], P(('group', 'dev')), may hold values from -100 to 100
- query_rope: bfloat16 [512, 128, 64], P(('group', 'dev')), may hold values from -3 to 3
- cache_latent: bfloat16 [512, 2048, 512], P(('group', 'dev')), may hold values from -6 to 6
- cache_rope: bfloat16 [512, 64, 2048], P(('group', 'dev')), may hold values from -6 to 6
- lengths: int32 [512], P(('group', 'dev')), may hold values from 256 to 2048
- value_up: bfloat16 [128, 512, 128], P('dev'), may hold values from -0.25 to 0.25
- out_proj: bfloat16 [16384, 7168], P('dev'), may hold values from -0.046875 to 0.046875
- residual: bfloat16 [512, 7168], P(('group', 'dev')), may hold values from -6 to 6
- norm_gain: float32 [7168], replicated, may hold values from 0.25 to 1.75
- expert_ids: int32 [512, 8], P(('group', 'dev')), may hold values from 0 to 31, all different within a row; in each aligned block of 4 rows (0 to 3, 4 to 7, ...) at most 2 rows name the same one
- gate_values: float32 [512, 8], P(('group', 'dev')), may hold values from 0.1 to 1
- w_gate: bfloat16 [64, 7168, 512], P('dev', None, 'group'), may hold values from -0.0625 to 0.0625
- w_up: bfloat16 [64, 7168, 512], P('dev', None, 'group'), may hold values from -0.0625 to 0.0625
- w_down: bfloat16 [64, 512, 7168], P('dev', 'group'), may hold values from -0.1875 to 0.1875
Outputs:
- layer_out: bfloat16 [512, 7168], P(('group', 'dev'))
Inputs may be any that keep to these rules, and one draw needn't show every extreme that they name: `expert_ids`: each row names 8 different experts. Among the rows of one device no expert is named by more than 2 rows, and in every draw some expert is named by exactly 2 rows of some device.
All inputs are finite; a program needn't handle non-finite values.
Results may differ from a plain program's by a relative error of at most 0.008.
Values may be sent and summed in bfloat16 or wider, within the bound.
A program may use at most 128 MiB of HBM per device.

v0:
```python
import jax
import jax.numpy as jnp
from jax import lax
from jax.sharding import Mesh
from jax.sharding import PartitionSpec as P

DEV = ("dev_0", "dev_1", "dev_2", "dev_3")
GROUP_DEV = ("group", "dev_0", "dev_1", "dev_2", "dev_3")
softmax_scale = 192.0 ** (-0.5)


def attend(query_latent, query_rope, cache_latent, cache_rope, lengths):
    scores = jnp.einsum(
        "thl,tcl->thc", query_latent, cache_latent, preferred_element_type=jnp.float32
    )
    scores = scores + jnp.einsum(
        "thr,trc->thc", query_rope, cache_rope, preferred_element_type=jnp.float32
    )
    scores = scores * softmax_scale
    positions = lax.broadcasted_iota(jnp.int32, scores.shape, 2)
    scores = jnp.where(positions < lengths[:, None, None], scores, -jnp.inf)
    row_peak = jnp.max(scores, axis=2, keepdims=True)
    weights = jnp.exp(scores - row_peak)
    attn_weights = (weights / jnp.sum(weights, axis=2, keepdims=True)).astype(jnp.bfloat16)
    return jnp.einsum(
        "thc,tcl->thl", attn_weights, cache_latent, preferred_element_type=jnp.float32
    ).astype(jnp.bfloat16)


def expert_rows(token_rows, w_gate, w_up, w_down):
    gate_part = jnp.dot(token_rows, w_gate[0], preferred_element_type=jnp.float32)
    up_part = jnp.dot(token_rows, w_up[0], preferred_element_type=jnp.float32)
    active = (jax.nn.silu(gate_part) * up_part).astype(jnp.bfloat16)
    return jnp.dot(active, w_down[0], preferred_element_type=jnp.float32)


def local(
    query_latent,
    query_rope,
    cache_latent,
    cache_rope,
    lengths,
    value_up,
    out_proj,
    residual,
    norm_gain,
    expert_ids,
    gate_values,
    w_gate,
    w_up,
    w_down,
):
    tok_rows = query_latent.shape[0]
    feature_width = residual.shape[1]
    mixed_latent = attend(query_latent, query_rope, cache_latent, cache_rope, lengths)
    by_head = lax.all_to_all(mixed_latent, DEV, split_axis=1, concat_axis=0, tiled=True)
    head_values = jnp.einsum(
        "thl,hlv->thv", by_head, value_up, preferred_element_type=jnp.float32
    ).astype(jnp.bfloat16)
    flat_values = head_values.reshape(head_values.shape[0], -1)
    attention_part = jnp.dot(flat_values, out_proj, preferred_element_type=jnp.float32)
    attention = lax.psum_scatter(
        attention_part.astype(jnp.bfloat16), DEV, scatter_dimension=0, tiled=True
    ).astype(jnp.float32)
    stream = residual.astype(jnp.float32) + attention
    normed = (
        stream * lax.rsqrt(jnp.mean(stream * stream, axis=1, keepdims=True) + 1e-06) * norm_gain
    ).astype(jnp.bfloat16)
    experts = lax.axis_size(DEV) // 2
    expert_range = jnp.arange(experts, dtype=jnp.int32)
    chosen = expert_ids[:, :, None] == expert_range[None, None, :]
    row_gates = jnp.sum(jnp.where(chosen, gate_values[:, :, None], 0.0), axis=1)
    all_rows = lax.all_gather(normed, GROUP_DEV, axis=0, tiled=True)
    all_gates = lax.all_gather(row_gates, GROUP_DEV, axis=0, tiled=True)
    mine = lax.axis_index(DEV) // 2
    my_gates = jnp.sum(jnp.where(expert_range[None, :] == mine, all_gates, 0.0), axis=1)
    partial_value = expert_rows(all_rows, w_gate, w_up, w_down) * my_gates[:, None]
    mixture = lax.psum_scatter(
        partial_value.astype(jnp.bfloat16), GROUP_DEV, scatter_dimension=0, tiled=True
    ).astype(jnp.float32)
    return (stream + mixture).astype(jnp.bfloat16)


def solution(mesh):
    finer = Mesh(
        mesh.devices.reshape(mesh.shape["group"], 4, 2, 4, 2),
        ("group", "dev_0", "dev_1", "dev_2", "dev_3"),
    )
    return jax.shard_map(
        local,
        mesh=finer,
        in_specs=(
            P(GROUP_DEV, None, None),
            P(GROUP_DEV, None, None),
            P(GROUP_DEV, None, None),
            P(GROUP_DEV, None, None),
            P(GROUP_DEV),
            P(DEV, None, None),
            P(DEV, None),
            P(GROUP_DEV, None),
            P(),
            P(GROUP_DEV, None),
            P(GROUP_DEV, None),
            P(DEV, None, "group"),
            P(DEV, None, "group"),
            P(DEV, "group", None),
        ),
        out_specs=P(GROUP_DEV, None),
        check_vma=False,
    )
```

profile of v0, /device:TPU:1, one launch (start us, length us, event | category | flops | bytes accessed | tf_op | source)
XLA Modules:
  0.0 1019.2 jit_solution(3751967246180345959)
XLA Ops:
  6.5 1.2 copy-done
  7.8 1.6 fusion.22
  9.4 6.3 multiply_select_fusion
  15.7 1.9 copy-done.2
  17.6 0.8 fusion.21
  18.4 7.6 fusion.8
  26.0 0.4 copy.20
  26.4 23.2 %all_to_all.18 = bf16[4,128,512]{2,0,1:T(4,128)(2,1)S(1)} all-to-all(bf16[4,128,512]{2,0,1:T(4,128)(2,1)S(1)} %copy.20), channel_id=1, replica_groups=mesh['group'=2,'dev_0'=4,'dev_1'=2,'dev_2'=4,'dev_3'=2] {'dev_0','dev_1'..., dimensions={1} | all-to-all | bytes 1048576 | tf_op jit(solution)/shard_map/all_to_all | solution.py:56
  49.6 0.2 copy.25
  49.8 0.1 all_to_all.16
  49.9 0.3 convolution_convert_fusion.1
  50.3 5.0 convolution_convert_fusion
  55.4 0.6 dynamic-slice
  56.7 557.5 %all-reduce.5.cloned.1.call-done = bf16[256,7168]{1,0:T(8,128)(2,1)} async-done(((bf16[256,7168]{1,0:T(8,128)(2,1)}), bf16[256,7168]{1,0:T(8,128)(2,1)}) %all-reduce.5.cloned.1.call-update) | async-done | bytes 3670032
  614.1 1.1 multiply_reduce_fusion
  615.2 1.6 fusion.18
  617.0 177.6 %all-gather.1 = f32[128,4,32]{2,1,0:T(4,128)S(1)} all-gather(f32[1,4,32]{2,1,0:T(4,128)S(1)} %bitcast.46), channel_id=1, replica_groups=mesh['group'=2,'dev_0'=4,'dev_1'=2,'dev_2'=4,'dev_3'=2] {'group','dev_0'..., dimensions={0}, use_global_device_ids=true | all-gather | bytes 66048 | tf_op jit(solution)/shard_map/all_gather | solution.py:74
  794.6 0.1 select_reduce_fusion
  794.8 23.3 %all-gather.4.cloned.1.call-done = bf16[128,4,7168]{2,1,0:T(4,128)(2,1)} async-done(((bf16[1,4,7168]{2,1,0:T(4,128)(2,1)}), bf16[128,4,7168]{2,1,0:T(4,128)(2,1)}) %all-gather.4.cloned.1.call-update) | async-done | bytes 7340048 | tf_op jit(solution)/shard_map/all_gather | solution.py:73
  818.1 12.1 %reshape.25 = bf16[512,7168]{1,0:T(8,128)(2,1)} reshape(bf16[128,4,7168]{2,1,0:T(4,128)(2,1)} %all-gather.4.cloned.1.call-done) | data formatting | bytes 14680064
  830.2 6.2 fusion.4
  836.4 16.1 %multiply_convert_fusion = bf16[512,7168]{1,0:T(8,128)(2,1)} fusion(f32[512]{0:T(512)S(1)} %select_reduce_fusion, bf16[1,256,7168]{2,1,0:T(8,128)(2,1)} %param.27, bf16[512,7168]{1,0:T(8,128)(2,1)} %reshape.25, bf16[1,7168,256]{2,1,0:T(8,128)(2,1)} %param.26, f32[512,256]{1,0:T(8,128)S(1)} %fusion.4), kind=kOutput, calls=%fused_computation.1 | convolution fusion | flops 3766222848 | bytes 22546432 | tf_op jit(solution)/shard_map/dot_general | solution.py:34
  852.5 158.5 %all-reduce.7.cloned.1.call-done = bf16[512,7168]{1,0:T(8,128)(2,1)} async-done(((bf16[512,7168]{1,0:T(8,128)(2,1)}), bf16[512,7168]{1,0:T(8,128)(2,1)}) %all-reduce.7.cloned.1.call-update) | async-done | bytes 7340048
  1011.1 1.7 add_convert_fusion
  (29 shorter events, 0.3 us)
Async XLA Ops:
  6.5 1.2 copy-start
  6.5 2.8 copy-start.9
  6.5 2.8 copy-start.3
  6.5 607.6 %all-reduce.5.cloned.1.call-start = ((), (), s32[]{:S(2)}) async-start(), calls=%async_computation.2 | async-start | bytes 7340032
  15.7 1.9 copy-start.2
  26.0 23.9 %copy-start.5 = (bf16[2,512,128]{2,1,0:T(8,128)(2,1)S(1)}, bf16[2,512,128]{2,1,0:T(8,128)(2,1)}, u32[]{:S(2)}) copy-start(bf16[2,512,128]{2,1,0:T(8,128)(2,1)} %param.19) | copy-start | bytes 786436
  50.3 5.2 copy-start.10
  50.3 563.8 %copy-start.4 = (bf16[4,7168]{1,0:T(4,128)(2,1)S(1)}, bf16[4,7168]{1,0:T(4,128)(2,1)}, u32[]{:S(2)}) copy-start(bf16[4,7168]{1,0:T(4,128)(2,1)} %param.21) | copy-start | bytes 172036
  50.3 564.9 %copy-start.6 = (f32[7168]{0:T(1024)S(1)}, f32[7168]{0:T(1024)}, u32[]{:S(2)}) copy-start(f32[7168]{0:T(1024)} %param.22) | copy-start | bytes 86020
  50.3 566.6 %copy-start.7 = (f32[4,8]{1,0:T(4,128)S(1)}, f32[4,8]{1,0:T(4,128)}, u32[]{:S(2)}) copy-start(f32[4,8]{1,0:T(4,128)} %param.24) | copy-start | bytes 388
  50.3 566.6 %copy-start.8 = (s32[4,8]{1,0:T(4,128)S(1)}, s32[4,8]{1,0:T(4,128)}, u32[]{:S(2)}) copy-start(s32[4,8]{1,0:T(4,128)} %param.23) | copy-start | bytes 388
  55.4 762.8 %all-gather.4.cloned.1.call-start = ((), (), s32[]{:S(2)}) async-start(), calls=%async_computation.1 | async-start | bytes 7397376 | tf_op jit(solution)/shard_map/all_gather | solution.py:73
  616.9 394.2 %all-reduce.7.cloned.1.call-start = ((), (), s32[]{:S(2)}) async-start(), calls=%async_computation.3 | async-start | bytes 14680064
  836.4 176.3 %copy-start.1 = (bf16[4,64,2048]{2,1,0:T(8,128)(2,1)S(1)}, bf16[4,64,2048]{2,1,0:T(8,128)(2,1)}, u32[]{:S(2)}) copy-start(bf16[4,64,2048]{2,1,0:T(8,128)(2,1)} %param.17) | copy-start | bytes 3145732
Sparse Core Ops, SparseCore 0:
  55.5 558.5 all-reduce.4
  617.0 201.1 all-gather.3
  852.7 158.3 all-reduce.6
where the time goes:
time: 1020 us
  waiting for transfers between devices  739 us (72%)
  blocking collectives  201 us (20%)
  matrix products  43.1 us (4%)
  local copies, waits for them, and re-layouts  16.6 us (2%)
  between operations  14 us (1%)
    unnamed x5, waiting for transfers between devices  716 us
    all_gather x1, blocking collectives, local(): all_gates = lax.all_gather(row_gates, GROUP_DEV, axis=0, tiled=True)  178 us
    all_gather x1, waiting for transfers between devices, local(): all_rows = lax.all_gather(normed, GROUP_DEV, axis=0, tiled=True)  23.3 us
    all_to_all x1, blocking collectives, local(): lax.all_to_all(mixed_latent, DEV, split_axis=1, concat_axis=0, tiled=True)  23.2 us
  transfers between devices with their start and end apart: 3, of which 3 were waited for; matrix products, arithmetic and copies ran while one was open for 0% of the time, Pallas kernels for 0%

commit v1 on v0

--- a/solution.py
+++ b/solution.py
@@ -7,6 +7,12 @@
 DEV = ("dev_0", "dev_1", "dev_2", "dev_3")
 GROUP_DEV = ("group", "dev_0", "dev_1", "dev_2", "dev_3")
 softmax_scale = 192.0 ** (-0.5)
+
+
+def _resolve_node(local_x, s0):
+    res = jnp.concatenate([local_x, s0], 1)
+    field_out = lax.all_gather(res, axis_name=GROUP_DEV, tiled=True, axis=0)
+    return jnp.split(field_out, [local_x.shape[1]], 1)
 
 
 def attend(query_latent, query_rope, cache_latent, cache_rope, lengths):
@@ -70,8 +76,7 @@
     expert_range = jnp.arange(experts, dtype=jnp.int32)
     chosen = expert_ids[:, :, None] == expert_range[None, None, :]
     row_gates = jnp.sum(jnp.where(chosen, gate_values[:, :, None], 0.0), axis=1)
-    all_rows = lax.all_gather(normed, GROUP_DEV, axis=0, tiled=True)
-    all_gates = lax.all_gather(row_gates, GROUP_DEV, axis=0, tiled=True)
+    all_rows, all_gates = _resolve_node(normed, row_gates)
     mine = lax.axis_index(DEV) // 2
     my_gates = jnp.sum(jnp.where(expert_range[None, :] == mine, all_gates, 0.0), axis=1)
     partial_value = expert_rows(all_rows, w_gate, w_up, w_down) * my_gates[:, None]

time: 1020 us -> 1040 us (1.020)
  waiting for transfers between devices: 739 us -> 926 us
  blocking collectives: 201 us -> 23.2 us
    all_gather x1, waiting for transfers between devices: 23.3 us -> 210 us  [_resolve_node(): field_out = lax.all_gather(res, axis_name=GROUP_DEV, tiled=True, axis=0)]
    all_gather x1 -> x0, blocking collectives: 178 us -> none  [local(): all_gates = lax.all_gather(row_gates, GROUP_DEV, axis=0, tiled=True)]
where the time goes in v1:
time: 1040 us
  waiting for transfers between devices  926 us (89%)
  matrix products  47.2 us (5%)
  blocking collectives  23.2 us (2%)
  local copies, waits for them, and re-layouts  22 us (2%)
  between operations  14 us (1%)
    unnamed x5, waiting for transfers between devices  716 us
    all_gather x1, waiting for transfers between devices, _resolve_node(): field_out = lax.all_gather(res, axis_name=GROUP_DEV, tiled=True, axis=0)  210 us
    all_to_all x1, blocking collectives, local(): lax.all_to_all(mixed_latent, DEV, split_axis=1, concat_axis=0, tiled=True)  23.2 us
    unnamed x24, local copies, waits for them, and re-layouts  21.3 us
  transfers between devices with their start and end apart: 3, of which 3 were waited for; matrix products, arithmetic and copies ran while one was open for 0% of the time, Pallas kernels for 0%

profile of v1, /device:TPU:1, one launch (start us, length us, event | category | flops | bytes accessed | tf_op | source)
XLA Modules:
  0.0 1039.3 jit_solution(1325345807390456826)
XLA Ops:
  6.5 1.2 copy-done
  7.8 1.6 fusion.30
  9.4 6.3 multiply_select_fusion
  15.7 1.9 copy-done.2
  17.6 0.8 fusion.29
  18.4 7.6 fusion.10
  26.0 0.4 copy.22
  26.4 23.2 %all_to_all.18 = bf16[4,128,512]{2,0,1:T(4,128)(2,1)S(1)} all-to-all(bf16[4,128,512]{2,0,1:T(4,128)(2,1)S(1)} %copy.22), channel_id=1, replica_groups=mesh['group'=2,'dev_0'=4,'dev_1'=2,'dev_2'=4,'dev_3'=2] {'dev_0','dev_1'..., dimensions={1} | all-to-all | bytes 1048576 | tf_op jit(solution)/shard_map/all_to_all | solution.py:62
  49.6 0.2 copy.27
  49.9 0.3 convolution_convert_fusion.1
  50.3 5.0 convolution_convert_fusion
  55.4 0.6 dynamic-slice
  56.8 557.3 %all-reduce.5.cloned.1.call-done = bf16[256,7168]{1,0:T(8,128)(2,1)} async-done(((bf16[256,7168]{1,0:T(8,128)(2,1)}), bf16[256,7168]{1,0:T(8,128)(2,1)}) %all-reduce.5.cloned.1.call-update) | async-done | bytes 3670032
  614.1 1.1 multiply_reduce_fusion
  615.2 1.0 fusion.26
  616.2 0.7 maximum_bitcast_fusion
  616.9 0.2 all-reduce.7.cloned.1.call-start
  617.2 210.2 %all-gather.3.cloned.1.call-done = f32[128,4,7200]{2,1,0:T(4,128)} async-done(((f32[1,4,7200]{2,1,0:T(4,128)}), f32[128,4,7200]{2,1,0:T(4,128)}) %all-gather.3.cloned.1.call-update) | async-done | bytes 14745616 | tf_op jit(solution)/shard_map/all_gather | solution.py:14
  827.3 17.5 %reshape.25 = f32[512,7200]{1,0:T(8,128)} reshape(f32[128,4,7200]{2,1,0:T(4,128)} %all-gather.3.cloned.1.call-done) | data formatting | bytes 29491200
  844.8 1.1 fusion.21
  845.9 8.3 fusion.3
  854.2 18.2 %multiply_convert_fusion = bf16[512,7168]{1,0:T(8,128)(2,1)} fusion(f32[512]{0:T(512)S(1)} %fusion.21, bf16[1,256,7168]{2,1,0:T(8,128)(2,1)} %param.27, bf16[1,7168,256]{2,1,0:T(8,128)(2,1)} %param.26, f32[512,7200]{1,0:T(8,128)} %reshape.25, f32[512,256]{1,0:T(8,128)S(1)} %fusion.3), kind=kOutput, calls=%fused_computation.1 | convolution fusion | flops 3766222848 | bytes 22546432 | tf_op jit(solution)/shard_map/dot_general | solution.py:40
  872.4 158.7 %all-reduce.7.cloned.1.call-done = bf16[512,7168]{1,0:T(8,128)(2,1)} async-done(((bf16[512,7168]{1,0:T(8,128)(2,1)}), bf16[512,7168]{1,0:T(8,128)(2,1)}) %all-reduce.7.cloned.1.call-update) | async-done | bytes 7340048
  1031.1 1.7 add_convert_fusion
  (29 shorter events, 0.4 us)
Async XLA Ops:
  6.5 1.2 copy-start
  6.5 2.8 copy-start.3
  6.5 2.8 copy-start.9
  6.5 607.6 %all-reduce.5.cloned.1.call-start = ((), (), s32[]{:S(2)}) async-start(), calls=%async_computation.2 | async-start | bytes 7340032
  15.7 1.9 copy-start.2
  26.0 23.9 %copy-start.5 = (bf16[2,512,128]{2,1,0:T(8,128)(2,1)S(1)}, bf16[2,512,128]{2,1,0:T(8,128)(2,1)}, u32[]{:S(2)}) copy-start(bf16[2,512,128]{2,1,0:T(8,128)(2,1)} %param.19) | copy-start | bytes 786436
  50.3 5.2 copy-start.10
  50.3 6.4 copy-start.7
  50.3 6.4 copy-start.8
  50.3 563.8 %copy-start.4 = (bf16[4,7168]{1,0:T(4,128)(2,1)S(1)}, bf16[4,7168]{1,0:T(4,128)(2,1)}, u32[]{:S(2)}) copy-start(bf16[4,7168]{1,0:T(4,128)(2,1)} %param.21) | copy-start | bytes 172036
  50.3 564.9 %copy-start.6 = (f32[7168]{0:T(1024)S(1)}, f32[7168]{0:T(1024)}, u32[]{:S(2)}) copy-start(f32[7168]{0:T(1024)} %param.22) | copy-start | bytes 86020
  55.4 772.0 %all-gather.3.cloned.1.call-start = ((), (), s32[]{:S(2)}) async-start(), calls=%async_computation.1 | async-start | bytes 15058944 | tf_op jit(solution)/shard_map/all_gather | solution.py:14
  616.9 414.2 %all-reduce.7.cloned.1.call-start = ((), (), s32[]{:S(2)}) async-start(), calls=%async_computation.3 | async-start | bytes 14680064
  854.2 178.5 %copy-start.1 = (bf16[4,64,2048]{2,1,0:T(8,128)(2,1)S(1)}, bf16[4,64,2048]{2,1,0:T(8,128)(2,1)}, u32[]{:S(2)}) copy-start(bf16[4,64,2048]{2,1,0:T(8,128)(2,1)} %param.17) | copy-start | bytes 3145732
Sparse Core Ops, SparseCore 0:
  55.5 558.5 all-reduce.4
  617.0 210.2 all-gather.2
  872.5 158.4 all-reduce.6
